TPU v7x, 32 devices: a whole 2x2x4 slice. The times are simulated.
32 devices in a mesh: loop: 8 (over z, core), red: 4 (over y, x).
Axes of the slice: x: 2, y: 2, z: 4, core: 2. Of those that a mesh axis runs over, the one named last changes fastest.
Arguments:
- query_ids: int32 [512], replicated, may hold values from 0 to 8191
- layer_index: int32 [1], replicated, may hold values from 0 to 3
- gradient: bfloat16 [8192, 28672], P('loop', 'red'), may hold values from -6 to 6
- out_basis: bfloat16 [8192, 8192], P('loop'), may hold values from -0.0625 to 0.0625
- in_basis: bfloat16 [28672, 28672], P('red', 'loop'), may hold values from -0.03125 to 0.03125
- out_eigen: float32 [4, 8192], replicated, may hold values from 0.2 to 2
- in_eigen: float32 [4, 28672], P(None, 'loop'), may hold values from 0.2 to 2
Outputs:
- preconditioned: bfloat16 [512, 28672], P('loop', 'red')
All inputs are finite; a program needn't handle non-finite values.
Results may differ from a plain program's by a relative error of at most 0.0055.
Values may be sent and summed in bfloat16 or wider, within the bound.
A program may use at most 192 MiB of HBM per device.

v0:
```python
import jax
import jax.numpy as jnp
from jax import lax
from jax.sharding import PartitionSpec as P

damping = 0.05


def per_device(query_ids, layer_index, gradient, out_basis, in_basis, out_eigen, in_eigen):
    selected = jnp.take(out_basis, query_ids, axis=1)
    shares = lax.psum_scatter(
        lax.dot_general(
            selected, gradient, (((0,), (0,)), ((), ())), preferred_element_type=jnp.float32
        ),
        "loop",
        scatter_dimension=0,
        tiled=True,
    )
    rows_w = lax.all_gather(shares.astype(jnp.bfloat16), "loop", axis=0, tiled=True)
    eigen_rows = jnp.take(jnp.take(out_eigen, layer_index, axis=0)[0], query_ids)
    eigen_cols = jnp.take(in_eigen, layer_index, axis=0)[0]
    local_rot = jnp.dot(rows_w, in_basis, preferred_element_type=jnp.float32)
    rotated = lax.psum(local_rot, "red")
    scaled = (rotated / (eigen_rows[:, None] * eigen_cols[None, :] + damping)).astype(jnp.bfloat16)
    result = lax.psum_scatter(
        lax.dot_general(
            scaled, in_basis, (((1,), (1,)), ((), ())), preferred_element_type=jnp.float32
        ),
        "loop",
        scatter_dimension=0,
        tiled=True,
    )
    return result.astype(jnp.bfloat16)


def solution(mesh):
    return jax.shard_map(
        per_device,
        mesh=mesh,
        in_specs=(
            P(),
            P(),
            P("loop", "red"),
            P("loop", None),
            P("red", "loop"),
            P(),
            P(None, "loop"),
        ),
        out_specs=P("loop", "red"),
        check_vma=False,
    )
```

profile of v0, /device:TPU:0, one launch (start us, length us, event | category | flops | bytes accessed | tf_op | source)
XLA Modules:
  0.0 673.3 jit_solution(5662324999065635593)
XLA Ops:
  6.5 0.0 reduce-scatter.3.cloned.1.call-start
  7.2 0.7 compare_select_fusion
  7.9 0.9 broadcast_select_fusion
  8.8 3.1 gather_fusion.1
  12.0 0.7 broadcast_select_fusion.2
  12.7 22.4 %copy.9 = bf16[1024,8192]{0,1:T(8,128)(2,1)} copy(bf16[1024,8192]{1,0:T(8,128)(2,1)} %param.10) | data formatting | bytes 33554432 | tf_op args[3]
  35.1 10.7 %gather_fusion = bf16[512,1024]{1,0:T(8,128)(2,1)S(1)} fusion(bf16[1024,8192]{0,1:T(8,128)(2,1)} %copy.9, s32[1024]{0:T(1024)S(1)} %pad_clamp_fusion), kind=kCustom, calls=%fused_computation | custom fusion | bytes 2099200 | tf_op jit(solution)/shard_map/jit(_take)/gather | solution.py:10
  45.8 16.3 %fusion.4 = f32[512,7168]{1,0:T(8,128)} fusion(bf16[1024,7168]{1,0:T(8,128)(2,1)} %param.9, bf16[512,1024]{1,0:T(8,128)(2,1)S(1)} %gather_fusion, pred[512]{0:T(512)(128)(4,1)S(1)} %get-tuple-element.28), kind=kOutput, calls=%fused_computation.7 | convolution fusion | flops 7516717056 | bytes 30409216 | tf_op jit(solution)/shard_map/dot_general | solution.py:12
  62.1 0.0 reduce-scatter.3.cloned.1.call-update
  62.1 0.0 all-gather.2.cloned.1.call-start
  62.2 151.8 %reduce-scatter.3.cloned.1.call-done = f32[64,7168]{1,0:T(8,128)} async-done(((f32[512,7168]{1,0:T(8,128)}), f32[64,7168]{1,0:T(8,128)}) %reduce-scatter.3.cloned.1.call-update) | async-done | bytes 1835024 | tf_op jit(solution)/shard_map/reduce_scatter | solution.py:11
  213.9 2.5 convert_element_type.9
  216.4 0.0 all-gather.2.cloned.1.call-update
  216.5 0.0 all-reduce.2.cloned.1.call-start
  216.5 71.9 %all-gather.2.cloned.1.call-done = bf16[512,7168]{1,0:T(8,128)(2,1)} async-done(((bf16[64,7168]{1,0:T(8,128)(2,1)}), bf16[512,7168]{1,0:T(8,128)(2,1)}) %all-gather.2.cloned.1.call-update) | async-done | bytes 7340048 | tf_op jit(solution)/shard_map/all_gather | solution.py:19
  288.5 35.4 %fusion.11 = f32[512,3584]{1,0:T(8,128)} fusion(bf16[512,7168]{1,0:T(8,128)(2,1)} %all-gather.2.cloned.1.call-done, bf16[7168,3584]{1,0:T(8,128)(2,1)} %param.11), kind=kOutput, calls=%fused_computation.20 | convolution fusion | flops 26306674688 | bytes 66060288 | tf_op jit(solution)/shard_map/dot_general | solution.py:22
  323.8 0.0 all-reduce.2.cloned.1.call-update
  323.9 0.2 reduce-scatter.5.cloned.1.call-start
  324.1 0.9 fusion.8
  325.0 153.0 %all-reduce.2.cloned.1.call-done = f32[512,3584]{1,0:T(8,128)} async-done(((f32[512,3584]{1,0:T(8,128)}), f32[512,3584]{1,0:T(8,128)}) %all-reduce.2.cloned.1.call-update) | async-done | bytes 7340048 | tf_op jit(solution)/shard_map/psum | solution.py:23
  478.0 37.1 %fusion = f32[512,7168]{1,0:T(8,128)} fusion(bf16[7168,3584]{1,0:T(8,128)(2,1)} %param.11, f32[512,3584]{1,0:T(8,128)} %all-reduce.2.cloned.1.call-done, f32[3584]{0:T(1024)S(1)} %fusion.8, f32[512]{0:T(512)S(1)} %get-tuple-element.27), kind=kOutput, calls=%fused_computation.3 | convolution fusion | flops 26314014720 | bytes 73416704 | tf_op jit(solution)/shard_map/dot_general | solution.py:26
  515.1 0.0 reduce-scatter.5.cloned.1.call-update
  515.2 149.1 %reduce-scatter.5.cloned.1.call-done = f32[64,7168]{1,0:T(8,128)} async-done(((f32[512,7168]{1,0:T(8,128)}), f32[64,7168]{1,0:T(8,128)}) %reduce-scatter.5.cloned.1.call-update) | async-done | bytes 1835024 | tf_op jit(solution)/shard_map/reduce_scatter | solution.py:25
  664.2 2.5 convert_element_type.11
  (1 shorter events, 0.0 us)
Async XLA Ops:
  6.5 207.4 %reduce-scatter.3.cloned.1.call-start = ((), (), s32[]{:S(2)}) async-start(), calls=%async_computation.2 | async-start | bytes 16515072 | tf_op jit(solution)/shard_map/reduce_scatter | solution.py:11
  62.1 226.3 %all-gather.2.cloned.1.call-start = ((), (), s32[]{:S(2)}) async-start(), calls=%async_computation.3 | async-start | bytes 8257536 | tf_op jit(solution)/shard_map/all_gather | solution.py:19
  216.5 261.5 %all-reduce.2.cloned.1.call-start = ((), (), s32[]{:S(2)}) async-start(), calls=%async_computation.4 | async-start | bytes 14680064 | tf_op jit(solution)/shard_map/psum | solution.py:23
  323.9 340.4 %reduce-scatter.5.cloned.1.call-start = ((), (), s32[]{:S(2)}) async-start(), calls=%async_computation.5 | async-start | bytes 16515072 | tf_op jit(solution)/shard_map/reduce_scatter | solution.py:25
Sparse Core Ops, SparseCore 0:
  62.2 151.6 reduce-scatter.2
  216.6 71.8 all-gather.1
  324.0 153.9 all-reduce.1
  515.3 148.9 reduce-scatter.4
where the time goes:
time: 674 us; the launch traced here: 673 us
  waiting for transfers between devices  526 us (78%)
  matrix products  88.8 us (13%)
  local copies, waits for them, and re-layouts  36.2 us (5%)
  between operations  13.8 us (2%)
  other arithmetic  8.23 us (1%)
    psum x1, waiting for transfers between devices, per_device(): rotated = lax.psum(local_rot, 'red')  153 us
    reduce_scatter x1, waiting for transfers between devices, per_device(): lax.psum_scatter(lax.dot_general(selected, gradient, (((0,), (0,)), ((),...  152 us
    reduce_scatter x1, waiting for transfers between devices, per_device(): lax.psum_scatter(lax.dot_general(scaled, in_basis, (((1,), (1,)), ((), ()...  149 us
    all_gather x1, waiting for transfers between devices, per_device(): lax.all_gather(shares.astype(jnp.bfloat16), 'loop', axis=0, tiled=True)  71.9 us
    dot_general x1, matrix products, per_device(): lax.dot_general(scaled, in_basis, (((1,), (1,)), ((), ())), preferred_ele...  37.1 us
    dot_general x1, matrix products, per_device(): local_rot = jnp.dot(rows_w, in_basis, preferred_element_type=jnp.float32)  35.4 us
    unnamed x1, local copies, waits for them, and re-layouts  22.4 us
    dot_general x1, matrix products, per_device(): lax.dot_general(selected, gradient, (((0,), (0,)), ((), ())), preferred_e...  16.3 us
  transfers between devices with their start and end apart: 4, of which 4 were waited for; matrix products, arithmetic and copies ran while one was open for 0% of the time, Pallas kernels for 0%

commit v1 on v0

--- a/solution.py
+++ b/solution.py
@@ -20,7 +20,11 @@
     eigen_rows = jnp.take(jnp.take(out_eigen, layer_index, axis=0)[0], query_ids)
     eigen_cols = jnp.take(in_eigen, layer_index, axis=0)[0]
     local_rot = jnp.dot(rows_w, in_basis, preferred_element_type=jnp.float32)
-    rotated = lax.psum(local_rot, "red")
+    peers = lax.axis_size("red")
+    rotated, hop = (local_rot, 1)
+    while hop < peers:
+        rotated = rotated + lax.ppermute(rotated, "red", [(i, i ^ hop) for i in range(peers)])
+        hop = 2 * hop
     scaled = (rotated / (eigen_rows[:, None] * eigen_cols[None, :] + damping)).astype(jnp.bfloat16)
     result = lax.psum_scatter(
         lax.dot_general(

time: 674 us -> 852 us (1.26)
  waiting for transfers between devices: 526 us -> 686 us
    ppermute x0 -> x2, waiting for transfers between devices: none -> 314 us  [per_device(): lax.ppermute(rotated, 'red', [(i, i ^ hop) for i in range(peers)])]
    psum x1 -> x0, waiting for transfers between devices: 153 us -> none  [per_device(): rotated = lax.psum(local_rot, 'red')]
    unnamed x1 -> x7, local copies, waits for them, and re-layouts: 22.4 us -> 29.7 us
  transfers between devices with their start and end apart: 4 -> 5, of which waited for: 4 -> 5; matrix products, arithmetic and copies ran while one was open for 0% -> 0% of each run, Pallas kernels for 0% -> 0%
where the time goes in v1:
time: 852 us; the launch traced here: 851 us
  waiting for transfers between devices  686 us (81%)
  matrix products  90 us (11%)
  local copies, waits for them, and re-layouts  43.5 us (5%)
  other arithmetic  14.7 us (2%)
  between operations  13.8 us (2%)
    ppermute x2, waiting for transfers between devices, per_device(): lax.ppermute(rotated, 'red', [(i, i ^ hop) for i in range(peers)])  314 us
    reduce_scatter x1, waiting for transfers between devices, per_device(): lax.psum_scatter(lax.dot_general(selected, gradient, (((0,), (0,)), ((),...  152 us
    reduce_scatter x1, waiting for transfers between devices, per_device(): lax.psum_scatter(lax.dot_general(scaled, in_basis, (((1,), (1,)), ((), ()...  148 us
    all_gather x1, waiting for transfers between devices, per_device(): lax.all_gather(shares.astype(jnp.bfloat16), 'loop', axis=0, tiled=True)  71.8 us
    dot_general x1, matrix products, per_device(): lax.dot_general(scaled, in_basis, (((1,), (1,)), ((), ())), preferred_ele...  41 us
    dot_general x1, matrix products, per_device(): local_rot = jnp.dot(rows_w, in_basis, preferred_element_type=jnp.float32)  32.6 us
    unnamed x7, local copies, waits for them, and re-layouts  29.7 us
  transfers between devices with their start and end apart: 5, of which 5 were waited for; matrix products, arithmetic and copies ran while one was open for 0% of the time, Pallas kernels for 0%

profile of v1, /device:TPU:0, one launch (start us, length us, event | category | flops | bytes accessed | tf_op | source)
XLA Modules:
  0.0 850.8 jit_solution(2398677097094739325)
XLA Ops:
  6.5 0.0 reduce-scatter.3.cloned.1.call-start
  7.2 0.7 compare_select_fusion
  7.9 0.9 broadcast_select_fusion
  8.8 3.1 gather_fusion.1
  12.0 0.7 broadcast_select_fusion.2
  12.7 22.4 %copy.9 = bf16[1024,8192]{0,1:T(8,128)(2,1)} copy(bf16[1024,8192]{1,0:T(8,128)(2,1)} %param.10) | data formatting | bytes 33554432 | tf_op args[3]
  35.1 10.7 %gather_fusion = bf16[512,1024]{1,0:T(8,128)(2,1)S(1)} fusion(bf16[1024,8192]{0,1:T(8,128)(2,1)} %copy.9, s32[1024]{0:T(1024)S(1)} %pad_clamp_fusion), kind=kCustom, calls=%fused_computation | custom fusion | bytes 2099200 | tf_op jit(solution)/shard_map/jit(_take)/gather | solution.py:10
  45.8 16.3 %fusion.4 = f32[512,7168]{1,0:T(8,128)} fusion(bf16[1024,7168]{1,0:T(8,128)(2,1)} %param.9, bf16[512,1024]{1,0:T(8,128)(2,1)S(1)} %gather_fusion, pred[512]{0:T(512)(128)(4,1)S(1)} %get-tuple-element.28), kind=kOutput, calls=%fused_computation.7 | convolution fusion | flops 7516717056 | bytes 30409216 | tf_op jit(solution)/shard_map/dot_general | solution.py:12
  62.1 0.0 reduce-scatter.3.cloned.1.call-update
  62.1 0.0 all-gather.2.cloned.1.call-start
  62.2 151.8 %reduce-scatter.3.cloned.1.call-done = f32[64,7168]{1,0:T(8,128)} async-done(((f32[512,7168]{1,0:T(8,128)}), f32[64,7168]{1,0:T(8,128)}) %reduce-scatter.3.cloned.1.call-update) | async-done | bytes 1835024 | tf_op jit(solution)/shard_map/reduce_scatter | solution.py:11
  213.9 2.5 convert_element_type.9
  216.4 0.0 all-gather.2.cloned.1.call-update
  216.5 0.2 reduce-scatter.5.cloned.1.call-start
  216.7 71.8 %all-gather.2.cloned.1.call-done = bf16[512,7168]{1,0:T(8,128)(2,1)} async-done(((bf16[64,7168]{1,0:T(8,128)(2,1)}), bf16[512,7168]{1,0:T(8,128)(2,1)}) %all-gather.2.cloned.1.call-update) | async-done | bytes 7340048 | tf_op jit(solution)/shard_map/all_gather | solution.py:19
  288.5 32.6 %fusion.11 = f32[512,3584]{1,0:T(8,128)S(1)} fusion(bf16[512,7168]{1,0:T(8,128)(2,1)} %all-gather.2.cloned.1.call-done, bf16[7168,3584]{1,0:T(8,128)(2,1)} %param.11), kind=kOutput, calls=%fused_computation.20 | convolution fusion | flops 26306674688 | bytes 66060288 | tf_op jit(solution)/shard_map/dot_general | solution.py:22
  321.1 0.0 copy-start.1
  321.1 1.5 collective-permute-start
  322.7 1.4 copy-done.1
  324.1 157.4 %collective-permute-done = f32[512,3584]{1,0:T(8,128)} collective-permute-done((f32[512,3584]{1,0:T(8,128)S(1)}, f32[512,3584]{1,0:T(8,128)}, u32[]{:S(2)}, u32[]{:S(2)}) %collective-permute-start) | collective-permute-done | bytes 7340064 | tf_op jit(solution)/shard_map/ppermute | solution.py:26
  481.4 6.5 add.36
  487.9 0.0 copy-start
  487.9 2.9 copy-done
  490.8 1.5 collective-permute-start.1
  492.3 0.9 fusion.8
  493.2 156.9 %collective-permute-done.1 = f32[512,3584]{1,0:T(8,128)S(1)} collective-permute-done((f32[512,3584]{1,0:T(8,128)S(1)}, f32[512,3584]{1,0:T(8,128)S(1)}, u32[]{:S(2)}, u32[]{:S(2)}) %collective-permute-start.1) | collective-permute-done | bytes 7340064 | tf_op jit(solution)/shard_map/ppermute | solution.py:26
  650.1 0.0 copy-start.2
  650.1 2.9 copy-done.2
  653.1 41.0 %fusion = f32[512,7168]{1,0:T(8,128)} fusion(bf16[7168,3584]{1,0:T(8,128)(2,1)} %param.11, f32[512,3584]{1,0:T(8,128)} %copy-done, f32[512,3584]{1,0:T(8,128)} %copy-done.2, f32[3584]{0:T(1024)S(1)} %fusion.8, f32[512]{0:T(512)S(1)} %get-tuple-element.27), kind=kOutput, calls=%fused_computation.3 | convolution fusion | flops 26315849728 | bytes 80756736 | tf_op jit(solution)/shard_map/dot_general | solution.py:30
  694.0 0.0 reduce-scatter.5.cloned.1.call-update
  694.1 147.7 %reduce-scatter.5.cloned.1.call-done = f32[64,7168]{1,0:T(8,128)} async-done(((f32[512,7168]{1,0:T(8,128)}), f32[64,7168]{1,0:T(8,128)}) %reduce-scatter.5.cloned.1.call-update) | async-done | bytes 1835024 | tf_op jit(solution)/shard_map/reduce_scatter | solution.py:29
  841.7 2.5 convert_element_type.11
  (1 shorter events, 0.0 us)
Async XLA Ops:
  6.5 207.4 %reduce-scatter.3.cloned.1.call-start = ((), (), s32[]{:S(2)}) async-start(), calls=%async_computation.2 | async-start | bytes 16515072 | tf_op jit(solution)/shard_map/reduce_scatter | solution.py:11
  62.1 226.3 %all-gather.2.cloned.1.call-start = ((), (), s32[]{:S(2)}) async-start(), calls=%async_computation.3 | async-start | bytes 8257536 | tf_op jit(solution)/shard_map/all_gather | solution.py:19
  216.5 625.3 %reduce-scatter.5.cloned.1.call-start = ((), (), s32[]{:S(2)}) async-start(), calls=%async_computation.4 | async-start | bytes 16515072 | tf_op jit(solution)/shard_map/reduce_scatter | solution.py:29
  321.1 3.0 copy-start.1
  321.1 160.3 %collective-permute-start = (f32[512,3584]{1,0:T(8,128)S(1)}, f32[512,3584]{1,0:T(8,128)}, u32[]{:S(2)}, u32[]{:S(2)}) collective-permute-start(f32[512,3584]{1,0:T(8,128)S(1)} %fusion.11), channel_id=1, source_target_pairs={{0,1},{1,0},{2,3},{3,2},{4,5},{5,4},{6,7},{7,6},{8,9},{9,8},{10,11... | collective-permute-start | bytes 22020104 | tf_op jit(solution)/shard_map/ppermute | solution.py:26
  487.9 2.9 copy-start
  490.8 159.3 %collective-permute-start.1 = (f32[512,3584]{1,0:T(8,128)S(1)}, f32[512,3584]{1,0:T(8,128)S(1)}, u32[]{:S(2)}, u32[]{:S(2)}) collective-permute-start(f32[512,3584]{1,0:T(8,128)S(1)} %add.36), channel_id=1, source_target_pairs={{0,2},{1,3},{2,0},{3,1},{4,6},{5,7},{6,4},{7,5},{8,10},{9,11},{10,... | collective-permute-start | bytes 22020104 | tf_op jit(solution)/shard_map/ppermute | solution.py:26
  650.1 3.0 copy-start.2
Sparse Core Ops, SparseCore 0:
  62.2 151.6 reduce-scatter.2
  216.6 71.8 all-gather.1
  694.2 147.4 reduce-scatter.4
